TPU v7x, 32 devices: a whole 2x2x4 slice. The times are simulated.
32 devices in a mesh: segment: 4 (over x, core), mp: 8 (over z, y).
Axes of the slice: x: 2, y: 2, z: 4, core: 2. Of those that a mesh axis runs over, the one named last changes fastest.
Arguments:
- frames_in: bfloat16 [1024, 1536], P('mp'), may hold values from -6 to 6
- section_weights: bfloat16 [4, 1536, 1536], P('segment', 'mp'), may hold values from -0.15625 to 0.15625
- conv_kernels: bfloat16 [4, 31, 1536], P('segment'), may hold values from -1 to 1
- valid_length: int32 [1], replicated, may hold values from 512 to 1024
- out_cotangent: bfloat16 [1024, 1536], P('mp'), may hold values from -6 to 6
Outputs:
- section_outputs: bfloat16 [4, 1024, 1536], P('segment', 'mp')
- input_grads: bfloat16 [4, 1024, 1536], P('segment', 'mp')
- kernel_grads: float32 [4, 31, 1536], P('segment', None, 'mp')
All inputs are finite; a program needn't handle non-finite values.
Results may differ from a plain program's by a relative error of at most 0.012.
Values may be sent and summed in bfloat16 or wider, within the bound.
A program may use at most 128 MiB of HBM per device.

v0:
```python
import functools

import jax
import jax.numpy as jnp
from jax import lax
from jax.experimental import pallas as pl
from jax.experimental.pallas import tpu as pltpu
from jax.sharding import PartitionSpec as P

EPSILON = 1e-05
PAD = 16
LANES = 128
ROWS = 16
WIDE = 256
MESH = pl.DeviceIdType.MESH
BF = jnp.bfloat16
F32 = jnp.float32


def cascade(
    x_ref, w_ref, k_ref, vl_ref, cot_ref,
    out_ref, gin_ref, kg_ref,
    cur, up, norm, inv, pm, pg, act, slope, gs,
    halo_send, halo_recv, in_send, in_recv, up_send, up_recv,
):
    frames, width = x_ref.shape
    taps = k_ref.shape[0]
    seg, mp = lax.axis_index("segment"), lax.axis_index("mp")
    n_seg, n_mp = lax.axis_size("segment"), lax.axis_size("mp")
    chunks = width // LANES
    blocks = frames // ROWS
    tiles = width // WIDE

    barrier = pltpu.get_barrier_semaphore()
    for axis, index, count in (("segment", seg, n_seg), ("mp", mp, n_mp)):
        for by in (1, count - 1):
            pl.semaphore_signal(
                barrier, inc=1, device_id={axis: lax.rem(index + by, count)}, device_id_type=MESH
            )
    pl.semaphore_wait(barrier, 4)

    def halo_copy(pad_ref, first, to_right):
        rows_from = pl.ds(frames, PAD) if to_right else pl.ds(PAD, PAD)
        rows_to = pl.ds(0, PAD) if to_right else pl.ds(frames + PAD, PAD)
        target = lax.rem(mp + (1 if to_right else n_mp - 1), n_mp)
        slot = first + (0 if to_right else 1)
        return pltpu.make_async_remote_copy(
            src_ref=pad_ref.at[rows_from], dst_ref=pad_ref.at[rows_to],
            send_sem=halo_send.at[slot], recv_sem=halo_recv.at[slot],
            device_id={"mp": target}, device_id_type=MESH,
        )

    def halo_start(pad_ref, first):
        @pl.when(mp < n_mp - 1)
        def _():
            halo_copy(pad_ref, first, True).start()

        @pl.when(mp > 0)
        def _():
            halo_copy(pad_ref, first, False).start()

    def halo_wait(pad_ref, first):
        @pl.when(mp > 0)
        def _():
            halo_copy(pad_ref, first, True).wait_recv()

        @pl.when(mp < n_mp - 1)
        def _():
            halo_copy(pad_ref, first, False).wait_recv()

    def halo_sent(pad_ref, first):
        @pl.when(mp < n_mp - 1)
        def _():
            halo_copy(pad_ref, first, True).wait_send()

        @pl.when(mp > 0)
        def _():
            halo_copy(pad_ref, first, False).wait_send()

    def halo_clear(pad_ref):
        @pl.when(mp == 0)
        def _():
            pad_ref[0:PAD, :] = jnp.zeros((PAD, width), BF)

        @pl.when(mp == n_mp - 1)
        def _():
            pad_ref[frames + PAD : frames + 2 * PAD, :] = jnp.zeros((PAD, width), BF)

    def in_copy(tile):
        columns = pl.ds(tile * WIDE, WIDE)
        return pltpu.make_async_remote_copy(
            src_ref=out_ref.at[:, columns], dst_ref=cur.at[:, columns],
            send_sem=in_send.at[tile], recv_sem=in_recv.at[tile],
            device_id={"segment": lax.rem(seg + 1, n_seg)}, device_id_type=MESH,
        )

    def up_copy(block):
        rows = pl.ds(block * ROWS, ROWS)
        return pltpu.make_async_remote_copy(
            src_ref=gin_ref.at[rows], dst_ref=up.at[rows],
            send_sem=up_send.at[block], recv_sem=up_recv.at[block],
            device_id={"segment": lax.rem(seg + n_seg - 1, n_seg)}, device_id_type=MESH,
        )

    def mask_rows(start, count):
        position = mp * frames + start + lax.broadcasted_iota(jnp.int32, (count, LANES), 0)
        return (position < vl_ref[0]).astype(F32)

    def back_product():
        for tile in range(tiles):
            columns = slice(tile * WIDE, (tile + 1) * WIDE)
            gs[:, columns] = lax.dot_general(
                up[...], w_ref[columns, :], (((1,), (1,)), ((), ())), preferred_element_type=F32
            )

    halo_clear(pm)
    halo_clear(pg)

    @pl.when(seg == n_seg - 1)
    def _():
        up[...] = cot_ref[...]
        back_product()

    @pl.when(seg == 0)
    def _():
        cur[...] = x_ref[...]

    @pl.when(seg > 0)
    def _():
        for tile in range(tiles):
            in_copy(tile).wait_recv()

    def norm_rows(block):
        start = pl.multiple_of(block * ROWS, ROWS)
        rows = pl.ds(start, ROWS)
        values = cur[rows, :].astype(F32)
        center = values - jnp.mean(values, axis=-1, keepdims=True)
        inverse = lax.rsqrt(jnp.mean(center * center, axis=-1, keepdims=True) + EPSILON)
        normed = center * inverse
        norm[rows, :] = normed
        inv[rows, :] = jnp.broadcast_to(inverse, (ROWS, LANES))
        pm[pl.ds(pl.multiple_of(PAD + start, ROWS), ROWS), :] = (
            normed * mask_rows(start, ROWS)[:, :1]
        ).astype(BF)

    norm_rows(0)
    norm_rows(blocks - 1)
    halo_start(pm, 0)

    @pl.loop(1, blocks - 1)
    def _(block):
        norm_rows(block)

    halo_wait(pm, 0)

    def shifted(padded):
        total = padded.shape[0]
        return [padded if r == 0 else pltpu.roll(padded, total - r, 0) for r in range(8)]

    def tap_sum(padded, columns, forward):
        total = padded.shape[0]
        running = jnp.zeros((frames, LANES), F32)
        for r in range(8):
            moved = padded if r == 0 else pltpu.roll(padded, total - r, 0)
            for base in range(0, 2 * PAD, 8):
                offset = base + r
                if 1 <= offset <= taps:
                    tap = offset - 1 if forward else taps - offset
                    running = running + k_ref[tap : tap + 1, columns] * moved[base : base + frames]
        return running

    @pl.loop(0, chunks)
    def _(chunk):
        columns = pl.ds(pl.multiple_of(chunk * LANES, LANES), LANES)
        conv = tap_sum(pm[:, columns].astype(F32), columns, True)
        gate = jax.nn.sigmoid(conv)
        act[:, columns] = (conv * gate).astype(BF)
        slope[:, columns] = gate * (1.0 + conv * (1.0 - gate))

    for tile in range(tiles):
        columns = slice(tile * WIDE, (tile + 1) * WIDE)
        product = jnp.dot(act[...], w_ref[:, columns], preferred_element_type=F32)
        out_ref[:, columns] = (cur[:, columns].astype(F32) + product).astype(BF)

        @pl.when(seg < n_seg - 1)
        def _():
            in_copy(tile).start()

    @pl.when(seg < n_seg - 1)
    def _():
        for block in range(blocks):
            up_copy(block).wait_recv()
        back_product()

    def grad_rows(block):
        start = pl.multiple_of(block * ROWS, ROWS)
        rows = pl.ds(start, ROWS)
        pg[pl.ds(pl.multiple_of(PAD + start, ROWS), ROWS), :] = (
            gs[rows, :] * slope[rows, :]
        ).astype(BF)

    grad_rows(0)
    grad_rows(blocks - 1)
    halo_start(pg, 2)

    @pl.loop(1, blocks - 1)
    def _(block):
        grad_rows(block)

    halo_wait(pg, 2)

    @pl.loop(0, chunks)
    def _(chunk):
        columns = pl.ds(pl.multiple_of(chunk * LANES, LANES), LANES)
        gs[:, columns] = tap_sum(pg[:, columns].astype(F32), columns, False) * mask_rows(0, frames)

    @pl.loop(0, blocks)
    def _(block):
        rows = pl.ds(pl.multiple_of(block * ROWS, ROWS), ROWS)
        masked = gs[rows, :]
        normed = norm[rows, :]
        first = jnp.mean(masked, axis=-1, keepdims=True)
        second = jnp.mean(masked * normed, axis=-1, keepdims=True)
        grad = inv[rows, :][:, :1] * (masked - first - normed * second)
        gin_ref[rows, :] = (up[rows, :].astype(F32) + grad).astype(BF)

        @pl.when(seg > 0)
        def _():
            up_copy(block).start()

    @pl.loop(0, chunks)
    def _(chunk):
        columns = pl.ds(pl.multiple_of(chunk * LANES, LANES), LANES)
        padded = pm[:, columns].astype(F32)
        grad = pg[PAD : PAD + frames, columns].astype(F32)
        total = padded.shape[0]
        for r in range(8):
            moved = padded if r == 0 else pltpu.roll(padded, total - r, 0)
            for base in range(0, 2 * PAD, 8):
                tap = base + r - 1
                if 0 <= tap < taps:
                    kg_ref[tap : tap + 1, columns] = jnp.sum(
                        grad * moved[base : base + frames], axis=0, keepdims=True
                    )

    halo_sent(pm, 0)
    halo_sent(pg, 2)

    @pl.when(seg < n_seg - 1)
    def _():
        for tile in range(tiles):
            in_copy(tile).wait_send()

    @pl.when(seg > 0)
    def _():
        for block in range(blocks):
            up_copy(block).wait_send()


def on_device(frames_in, section_weights, conv_kernels, valid_length, out_cotangent):
    frames, width = frames_in.shape
    taps = conv_kernels.shape[1]
    weight = lax.all_gather(section_weights[0], "mp", axis=0, tiled=True)
    vmem = pl.BlockSpec(memory_space=pltpu.VMEM)
    smem = pl.BlockSpec(memory_space=pltpu.SMEM)
    padded = (frames + 2 * PAD, width)
    dma = pltpu.SemaphoreType.DMA
    out, gin, part = pl.pallas_call(
        cascade,
        out_shape=(
            jax.ShapeDtypeStruct((frames, width), BF),
            jax.ShapeDtypeStruct((frames, width), BF),
            jax.ShapeDtypeStruct((taps, width), F32),
        ),
        in_specs=[vmem, vmem, vmem, smem, vmem],
        out_specs=(vmem, vmem, vmem),
        scratch_shapes=[
            pltpu.VMEM((frames, width), BF),
            pltpu.VMEM((frames, width), BF),
            pltpu.VMEM((frames, width), F32),
            pltpu.VMEM((frames, LANES), F32),
            pltpu.VMEM(padded, BF),
            pltpu.VMEM(padded, BF),
            pltpu.VMEM((frames, width), BF),
            pltpu.VMEM((frames, width), F32),
            pltpu.VMEM((frames, width), F32),
            dma((4,)), dma((4,)),
            dma((width // WIDE,)), dma((width // WIDE,)),
            dma((frames // ROWS,)), dma((frames // ROWS,)),
        ],
        compiler_params=pltpu.CompilerParams(
            collective_id=0, has_side_effects=True, vmem_limit_bytes=48 * 2**20
        ),
    )(frames_in, weight, conv_kernels[0].astype(F32), valid_length, out_cotangent)
    grad = lax.psum_scatter(part, "mp", scatter_dimension=1, tiled=True)
    grad = grad * (frames * lax.axis_size("mp")) ** (-0.5)
    return (out[None], gin[None], grad[None])


def solution(mesh):
    in_specs = (
        P("mp", None),
        P("segment", "mp", None),
        P("segment", None, None),
        P(),
        P("mp", None),
    )
    out_specs = (P("segment", "mp", None), P("segment", "mp", None), P("segment", None, "mp"))
    return jax.shard_map(
        on_device, mesh=mesh, in_specs=in_specs, out_specs=out_specs, check_vma=False
    )
```

profile of v0, /device:TPU:0, one launch (start us, length us, event | category | flops | bytes accessed | tf_op | source)
XLA Modules:
  0.0 251.7 jit_solution(2207410063277619065)
XLA Ops:
  7.2 0.0 all-gather.3.cloned.1.call-start
  7.2 0.7 all-gather.3.cloned.1.call-update
  7.9 0.0 reduce-scatter.4.cloned.1.call-start
  8.6 0.9 bitcast_convert_fusion.k_ref
  9.5 83.3 %all-gather.3.cloned.1.call-done = bf16[1,1536,1536]{2,1,0:T(8,128)(2,1)} async-done(((bf16[1,192,1536]{2,1,0:T(8,128)(2,1)}), bf16[1,1536,1536]{2,1,0:T(8,128)(2,1)}) %all-gather.3.cloned.1.call-update) | async-done | bytes 4718608 | tf_op jit(solution)/shard_map/all_gather | solution.py:263
  92.8 0.0 copy-start
  92.8 1.0 copy-done
  93.8 0.0 copy-start.1
  93.8 1.0 copy-done.1
  94.8 84.4 %shard_map.76 = (bf16[128,1536]{1,0:T(8,128)(2,1)S(1)}, bf16[128,1536]{1,0:T(8,128)(2,1)S(1)}, f32[31,1536]{1,0:T(8,128)S(1)}) custom-call(bf16[128,1536]{1,0:T(8,128)(2,1)S(1)} %copy-done, bf16[1536,1536]{1,0:T(8,128)(2,1)} %bitcast.12, f32[31,1536]{1,0:T(8,128)S(1)} %bitcast_convert_fusion.k_ref, s32[1]{0:T(128)S(6)} %copy.14.vl_ref, ...), custom_call_target="tpu_custom_call" | custom-call | tf_op jit(solution)/shard_map/pallas_call | solution.py:268
  179.2 1.2 copy.10
  180.4 0.0 reduce-scatter.4.cloned.1.call-update
  180.5 61.3 %reduce-scatter.4.cloned.1.call-done = f32[192,31]{1,0:T(8,128)} async-done(((f32[1536,31]{1,0:T(8,128)}), f32[192,31]{1,0:T(8,128)}) %reduce-scatter.4.cloned.1.call-update) | async-done | bytes 23824
  241.8 1.0 copy.11
  242.7 0.7 copy.9
  243.4 0.7 copy.15
  244.1 0.7 copy.16
  (1 shorter events, 0.0 us)
Async XLA Ops:
  7.2 85.6 %all-gather.3.cloned.1.call-start = ((), (), s32[]{:S(2)}) async-start(), calls=%async_computation.1 | async-start | bytes 5308416 | tf_op jit(solution)/shard_map/all_gather | solution.py:263
  7.9 233.9 %reduce-scatter.4.cloned.1.call-start = ((), (), s32[]{:S(2)}) async-start(), calls=%async_computation.2 | async-start | bytes 884736
  92.8 1.0 copy-start
  93.8 1.0 copy-start.1
Sparse Core Ops, SparseCore 0:
  10.2 82.5 all-gather.2
  180.6 61.1 reduce-scatter.3
where the time goes:
time: 252 us
  waiting for transfers between devices  145 us (58%)
  Pallas kernels  84.4 us (33%)
  between operations  14.7 us (6%)
  local copies, waits for them, and re-layouts  6.3 us (2%)
    pallas_call x1, Pallas kernels, on_device(): pl.pallas_call(cascade, out_shape=(jax.ShapeDtypeStruct((frames, width),...  84.4 us
    all_gather x1, waiting for transfers between devices, on_device(): weight = lax.all_gather(section_weights[0], 'mp', axis=0, tiled=True)  83.3 us
    unnamed x3, waiting for transfers between devices  62 us
    unnamed x9, local copies, waits for them, and re-layouts  6.3 us
  transfers between devices with their start and end apart: 2, of which 2 were waited for; matrix products, arithmetic and copies ran while one was open for 0% of the time, Pallas kernels for 0%

commit v1 on v0

--- a/solution.py
+++ b/solution.py
@@ -18,12 +18,14 @@
 
 
 def cascade(
-    x_ref, w_ref, k_ref, vl_ref, cot_ref,
-    out_ref, gin_ref, kg_ref,
-    cur, up, norm, inv, pm, pg, act, slope, gs,
+    relay, x_any, w_any, k_bf, vl_ref, cot_any,
+    out_whole, gin_whole, kg_out,
+    cur, up, norm, inv, pm, pg, act, slope, gs, w_ref, k_ref, kg_ref, kg_land,
     halo_send, halo_recv, in_send, in_recv, up_send, up_recv,
+    local_sem, w_send, w_recv, kg_send, kg_recv, turn_sem,
 ):
-    frames, width = x_ref.shape
+    out_ref, gin_ref = out_whole.at[0], gin_whole.at[0]
+    frames, width = x_any.shape
     taps = k_ref.shape[0]
     seg, mp = lax.axis_index("segment"), lax.axis_index("mp")
     n_seg, n_mp = lax.axis_size("segment"), lax.axis_size("mp")
@@ -32,12 +34,103 @@
     tiles = width // WIDE
 
     barrier = pltpu.get_barrier_semaphore()
-    for axis, index, count in (("segment", seg, n_seg), ("mp", mp, n_mp)):
-        for by in (1, count - 1):
+    steps_mp = range(1, n_mp) if relay else (1, n_mp - 1)
+    for axis, index, count, steps in (
+        ("segment", seg, n_seg, (1, n_seg - 1)), ("mp", mp, n_mp, steps_mp)
+    ):
+        for by in steps:
             pl.semaphore_signal(
                 barrier, inc=1, device_id={axis: lax.rem(index + by, count)}, device_id_type=MESH
             )
-    pl.semaphore_wait(barrier, 4)
+    own = width // n_mp
+    w_rows = pl.ds(pl.multiple_of(mp * own, own), own) if relay else pl.ds(0, width)
+    w_copy = pltpu.make_async_copy(w_any, w_ref.at[w_rows], local_sem.at[0])
+    x_copy = pltpu.make_async_copy(x_any, cur, local_sem.at[1])
+    cot_copy = pltpu.make_async_copy(cot_any, up, local_sem.at[2])
+    w_copy.start()
+
+    @pl.when(seg == 0)
+    def _():
+        x_copy.start()
+
+    @pl.when(seg == n_seg - 1)
+    def _():
+        cot_copy.start()
+
+    pl.semaphore_wait(barrier, 2 + len(steps_mp))
+
+    row, column = lax.div(mp, 2), lax.rem(mp, 2)
+    n_row = n_mp // 2
+
+    def block_copy(block, way):
+        rows = pl.ds(pl.multiple_of(block * own, own), own)
+        target = (mp + 2, mp - 2, mp + 1 - 2 * column)[way]
+        return pltpu.make_async_remote_copy(
+            src_ref=w_ref.at[rows], dst_ref=w_ref.at[rows],
+            send_sem=w_send.at[way, block], recv_sem=w_recv.at[block],
+            device_id={"mp": target}, device_id_type=MESH,
+        )
+
+    def each_block(distance, act_on, arrive):
+        if distance == 0:
+            pl.when(row < n_row - 1)(lambda: act_on(mp, 0))
+            pl.when(row > 0)(lambda: act_on(mp, 1))
+            act_on(mp, 2)
+            return
+        low, high = mp - 2 * distance, mp + 2 * distance
+
+        @pl.when(row >= distance)
+        def _():
+            arrive(low)
+            pl.when(row < n_row - 1)(lambda: act_on(low, 0))
+            act_on(low, 2)
+
+        @pl.when(row + distance < n_row)
+        def _():
+            arrive(high)
+            pl.when(row > 0)(lambda: act_on(high, 1))
+            act_on(high, 2)
+
+    def pass_on(distance):
+        each_block(
+            distance,
+            lambda block, way: block_copy(block, way).start(),
+            lambda block: block_copy(block, 0).wait_recv(),
+        )
+
+    def passed():
+        for distance in range(n_row):
+            each_block(
+                distance,
+                lambda block, way: block_copy(block, way).wait_send(),
+                lambda block: None,
+            )
+
+    def gather_rest(first):
+        if relay:
+            for distance in range(first, n_row):
+                pass_on(distance)
+            for index in range(n_row):
+                block_copy(index * 2 + 1 - column, 2).wait_recv()
+
+    def kg_copy(target, sender):
+        start = 384 * lax.div(target, 2) + 128 * lax.rem(target, 2)
+        window = pl.ds(pl.multiple_of(start, LANES), 2 * LANES)
+        return pltpu.make_async_remote_copy(
+            src_ref=kg_ref.at[:, window], dst_ref=kg_land.at[sender],
+            send_sem=kg_send.at[target], recv_sem=kg_recv.at[sender],
+            device_id={"mp": target}, device_id_type=MESH,
+        )
+
+    w_copy.wait()
+    if relay:
+
+        @pl.when(seg != 1)
+        def _():
+            pass_on(0)
+
+    k_ref[...] = k_bf[...].astype(F32)
+    kg_ref[...] = jnp.zeros(kg_ref.shape, F32)
 
     def halo_copy(pad_ref, first, to_right):
         rows_from = pl.ds(frames, PAD) if to_right else pl.ds(PAD, PAD)
@@ -118,12 +211,23 @@
 
     @pl.when(seg == n_seg - 1)
     def _():
-        up[...] = cot_ref[...]
+        gather_rest(1)
+        cot_copy.wait()
         back_product()
 
     @pl.when(seg == 0)
     def _():
-        cur[...] = x_ref[...]
+        x_copy.wait()
+
+    @pl.when(seg == 1)
+    def _():
+        if relay:
+            pl.semaphore_wait(turn_sem, 1)
+        gather_rest(0)
+
+    @pl.when((seg > 1) & (seg < n_seg - 1))
+    def _():
+        gather_rest(1)
 
     @pl.when(seg > 0)
     def _():
@@ -151,6 +255,12 @@
     def _(block):
         norm_rows(block)
 
+    if relay:
+
+        @pl.when(seg == 0)
+        def _():
+            pass_on(1)
+
     halo_wait(pm, 0)
 
     def shifted(padded):
@@ -177,6 +287,14 @@
         act[:, columns] = (conv * gate).astype(BF)
         slope[:, columns] = gate * (1.0 + conv * (1.0 - gate))
 
+    @pl.when(seg == 0)
+    def _():
+        gather_rest(2)
+        if relay:
+            pl.semaphore_signal(
+                turn_sem, inc=1, device_id={"segment": seg + 1}, device_id_type=MESH
+            )
+
     for tile in range(tiles):
         columns = slice(tile * WIDE, (tile + 1) * WIDE)
         product = jnp.dot(act[...], w_ref[:, columns], preferred_element_type=F32)
@@ -206,6 +324,33 @@
     @pl.loop(1, blocks - 1)
     def _(block):
         grad_rows(block)
+
+    kg_start = 384 * row + 128 * column
+    kg_window = pl.ds(pl.multiple_of(kg_start, LANES), 2 * LANES)
+
+    def tap_grads():
+        @pl.loop(0, chunks)
+        def _(chunk):
+            columns = pl.ds(pl.multiple_of(chunk * LANES, LANES), LANES)
+            padded = pm[:, columns].astype(F32)
+            grad = pg[PAD : PAD + frames, columns].astype(F32)
+            total = padded.shape[0]
+            for r in range(8):
+                moved = padded if r == 0 else pltpu.roll(padded, total - r, 0)
+                for base in range(0, 2 * PAD, 8):
+                    tap = base + r - 1
+                    if 0 <= tap < taps:
+                        kg_ref[tap : tap + 1, columns] = jnp.sum(
+                            grad * moved[base : base + frames], axis=0, keepdims=True
+                        )
+
+        if relay:
+            for by in range(1, n_mp):
+                kg_copy(lax.rem(mp + by, n_mp), mp).start()
+
+    @pl.when(seg == 0)
+    def _():
+        tap_grads()
 
     halo_wait(pg, 2)
 
@@ -228,20 +373,24 @@
         def _():
             up_copy(block).start()
 
-    @pl.loop(0, chunks)
-    def _(chunk):
-        columns = pl.ds(pl.multiple_of(chunk * LANES, LANES), LANES)
-        padded = pm[:, columns].astype(F32)
-        grad = pg[PAD : PAD + frames, columns].astype(F32)
-        total = padded.shape[0]
-        for r in range(8):
-            moved = padded if r == 0 else pltpu.roll(padded, total - r, 0)
-            for base in range(0, 2 * PAD, 8):
-                tap = base + r - 1
-                if 0 <= tap < taps:
-                    kg_ref[tap : tap + 1, columns] = jnp.sum(
-                        grad * moved[base : base + frames], axis=0, keepdims=True
-                    )
+    @pl.when(seg > 0)
+    def _():
+        tap_grads()
+
+    if relay:
+        total = kg_ref[:, kg_window]
+        for by in range(1, n_mp):
+            sender = lax.rem(mp + n_mp - by, n_mp)
+            kg_copy(mp, sender).wait_recv()
+            total = total + kg_land[sender]
+        scale = (frames * n_mp) ** (-0.5)
+        even, odd = total[:taps, :own], total[:taps, 2 * LANES - own :]
+        kg_out[0] = jnp.where(column == 0, even, odd) * scale
+        for by in range(1, n_mp):
+            kg_copy(lax.rem(mp + by, n_mp), mp).wait_send()
+        passed()
+    else:
+        kg_out[0] = kg_ref[:taps, :]
 
     halo_sent(pm, 0)
     halo_sent(pg, 2)
@@ -260,19 +409,26 @@
 def on_device(frames_in, section_weights, conv_kernels, valid_length, out_cotangent):
     frames, width = frames_in.shape
     taps = conv_kernels.shape[1]
-    weight = lax.all_gather(section_weights[0], "mp", axis=0, tiled=True)
+    n_mp = lax.axis_size("mp")
+    own = width // n_mp
+    relay = own == 192 and n_mp == 8
+    weight = section_weights[0]
+    if not relay:
+        weight = lax.all_gather(weight, "mp", axis=0, tiled=True)
     vmem = pl.BlockSpec(memory_space=pltpu.VMEM)
     smem = pl.BlockSpec(memory_space=pltpu.SMEM)
+    whole = pl.BlockSpec(memory_space=pl.ANY)
     padded = (frames + 2 * PAD, width)
+    tap_rows = -(-taps // 8) * 8
     dma = pltpu.SemaphoreType.DMA
-    out, gin, part = pl.pallas_call(
-        cascade,
+    out, gin, grad = pl.pallas_call(
+        functools.partial(cascade, relay),
         out_shape=(
-            jax.ShapeDtypeStruct((frames, width), BF),
-            jax.ShapeDtypeStruct((frames, width), BF),
-            jax.ShapeDtypeStruct((taps, width), F32),
+            jax.ShapeDtypeStruct((1, frames, width), BF),
+            jax.ShapeDtypeStruct((1, frames, width), BF),
+            jax.ShapeDtypeStruct((1, taps, own if relay else width), F32),
         ),
-        in_specs=[vmem, vmem, vmem, smem, vmem],
+        in_specs=[whole, whole, vmem, smem, whole],
         out_specs=(vmem, vmem, vmem),
         scratch_shapes=[
             pltpu.VMEM((frames, width), BF),
@@ -284,17 +440,25 @@
             pltpu.VMEM((frames, width), BF),
             pltpu.VMEM((frames, width), F32),
             pltpu.VMEM((frames, width), F32),
+            pltpu.VMEM((width, width), BF),
+            pltpu.VMEM((taps, width), F32),
+            pltpu.VMEM((tap_rows, width), F32),
+            pltpu.VMEM((n_mp if relay else 1, tap_rows, 2 * LANES), F32),
             dma((4,)), dma((4,)),
             dma((width // WIDE,)), dma((width // WIDE,)),
             dma((frames // ROWS,)), dma((frames // ROWS,)),
+            dma((3,)),
+            dma((3, n_mp)), dma((n_mp,)), dma((n_mp,)), dma((n_mp,)),
+            pltpu.SemaphoreType.REGULAR,
         ],
         compiler_params=pltpu.CompilerParams(
             collective_id=0, has_side_effects=True, vmem_limit_bytes=48 * 2**20
         ),
-    )(frames_in, weight, conv_kernels[0].astype(F32), valid_length, out_cotangent)
-    grad = lax.psum_scatter(part, "mp", scatter_dimension=1, tiled=True)
-    grad = grad * (frames * lax.axis_size("mp")) ** (-0.5)
-    return (out[None], gin[None], grad[None])
+    )(frames_in, weight, conv_kernels[0], valid_length, out_cotangent)
+    if not relay:
+        grad = lax.psum_scatter(grad, "mp", scatter_dimension=2, tiled=True)
+        grad = grad * (frames * n_mp) ** (-0.5)
+    return (out, gin, grad)
 
 
 def solution(mesh):

time: 252 us -> 153 us (0.61)
  waiting for transfers between devices: 145 us -> 0 us
  Pallas kernels: 84.4 us -> 145 us
  between operations: 14.7 us -> 1.3 us
    all_gather x1 -> x0, waiting for transfers between devices: 83.3 us -> none  [on_device(): weight = lax.all_gather(section_weights[0], 'mp', axis=0, tiled=True)]
    unnamed x3 -> x0, waiting for transfers between devices: 62 us -> none
    pallas_call x1, Pallas kernels: 84.4 us -> 145 us  [on_device(): pl.pallas_call(functools.partial(cascade, relay), out_shape=(jax.ShapeDty...]
    unnamed x9 -> x10, local copies, waits for them, and re-layouts: 6.3 us -> 5.43 us
  transfers between devices with their start and end apart: 2 -> 0, of which waited for: 2 -> 0; matrix products, arithmetic and copies ran while one was open for 0% -> 0% of each run, Pallas kernels for 0% -> 0%
where the time goes in v1:
time: 153 us; the launch traced here: 152 us
  Pallas kernels  145 us (95%)
  local copies, waits for them, and re-layouts  6.07 us (4%)
    pallas_call x1, Pallas kernels, on_device(): pl.pallas_call(functools.partial(cascade, relay), out_shape=(jax.ShapeDty...  145 us
    unnamed x10, local copies, waits for them, and re-layouts  5.43 us

profile of v1, /device:TPU:0, one launch (start us, length us, event | category | flops | bytes accessed | tf_op | source)
XLA Modules:
  0.0 152.2 jit_solution(14016896963271544715)
XLA Ops:
  1.3 0.0 copy-start
  1.3 1.1 copy-done
  2.3 0.0 copy-start.1
  2.3 1.0 copy-done.1
  3.3 0.0 copy-start.2
  3.3 1.0 copy-done.2
  4.3 0.0 copy-start.3
  4.3 0.9 copy-done.3
  5.2 144.9 %shard_map.76 = (bf16[1,128,1536]{2,1,0:T(8,128)(2,1)S(1)}, bf16[1,128,1536]{2,1,0:T(8,128)(2,1)S(1)}, f32[1,31,192]{2,1,0:T(8,128)S(1)}) custom-call(bf16[128,1536]{1,0:T(8,128)(2,1)S(1)} %copy-done.1, bf16[192,1536]{1,0:T(8,128)(2,1)S(1)} %bitcast.2, bf16[31,1536]{1,0:T(8,128)(2,1)S(1)} %bitcast.3, s32[1]{0:T(128)S(6)} %copy.11.vl_ref, ...), custom_call_target="tpu_custom_call" | custom-call | tf_op jit(solution)/shard_map/pallas_call | solution.py:424
  150.1 0.6 copy.8
  150.7 0.7 copy.12
  151.5 0.7 copy.13
Async XLA Ops:
  1.3 1.1 copy-start
  2.3 1.0 copy-start.1
  3.3 1.0 copy-start.2
  4.3 0.9 copy-start.3

commit v2 on v1

--- a/solution.py
+++ b/solution.py
@@ -18,9 +18,9 @@
 
 
 def cascade(
-    relay, x_any, w_any, k_bf, vl_ref, cot_any,
+    relay, x_any, w_any, k_any, vl_ref, cot_any,
     out_whole, gin_whole, kg_out,
-    cur, up, norm, inv, pm, pg, act, slope, gs, w_ref, k_ref, kg_ref, kg_land,
+    cur, up, norm, inv, pm, pg, act, slope, gs, w_ref, k_bf, k_ref, kg_ref, kg_land,
     halo_send, halo_recv, in_send, in_recv, up_send, up_recv,
     local_sem, w_send, w_recv, kg_send, kg_recv, turn_sem,
 ):
@@ -47,7 +47,9 @@
     w_copy = pltpu.make_async_copy(w_any, w_ref.at[w_rows], local_sem.at[0])
     x_copy = pltpu.make_async_copy(x_any, cur, local_sem.at[1])
     cot_copy = pltpu.make_async_copy(cot_any, up, local_sem.at[2])
+    k_copy = pltpu.make_async_copy(k_any, k_bf, local_sem.at[3])
     w_copy.start()
+    k_copy.start()
 
     @pl.when(seg == 0)
     def _():
@@ -129,6 +131,7 @@
         def _():
             pass_on(0)
 
+    k_copy.wait()
     k_ref[...] = k_bf[...].astype(F32)
     kg_ref[...] = jnp.zeros(kg_ref.shape, F32)
 
@@ -223,7 +226,7 @@
     def _():
         if relay:
             pl.semaphore_wait(turn_sem, 1)
-        gather_rest(0)
+            pass_on(0)
 
     @pl.when((seg > 1) & (seg < n_seg - 1))
     def _():
@@ -257,7 +260,7 @@
 
     if relay:
 
-        @pl.when(seg == 0)
+        @pl.when(seg < 2)
         def _():
             pass_on(1)
 
@@ -287,13 +290,21 @@
         act[:, columns] = (conv * gate).astype(BF)
         slope[:, columns] = gate * (1.0 + conv * (1.0 - gate))
 
-    @pl.when(seg == 0)
-    def _():
-        gather_rest(2)
-        if relay:
+    if relay:
+
+        @pl.when(seg < 2)
+        def _():
+            pass_on(2)
+
+        @pl.when(seg == 0)
+        def _():
             pl.semaphore_signal(
                 turn_sem, inc=1, device_id={"segment": seg + 1}, device_id_type=MESH
             )
+
+        @pl.when(seg < 2)
+        def _():
+            gather_rest(3)
 
     for tile in range(tiles):
         columns = slice(tile * WIDE, (tile + 1) * WIDE)
@@ -428,7 +439,7 @@
             jax.ShapeDtypeStruct((1, frames, width), BF),
             jax.ShapeDtypeStruct((1, taps, own if relay else width), F32),
         ),
-        in_specs=[whole, whole, vmem, smem, whole],
+        in_specs=[whole, whole, whole, smem, whole],
         out_specs=(vmem, vmem, vmem),
         scratch_shapes=[
             pltpu.VMEM((frames, width), BF),
@@ -441,18 +452,19 @@
             pltpu.VMEM((frames, width), F32),
             pltpu.VMEM((frames, width), F32),
             pltpu.VMEM((width, width), BF),
+            pltpu.VMEM((taps, width), BF),
             pltpu.VMEM((taps, width), F32),
             pltpu.VMEM((tap_rows, width), F32),
             pltpu.VMEM((n_mp if relay else 1, tap_rows, 2 * LANES), F32),
             dma((4,)), dma((4,)),
             dma((width // WIDE,)), dma((width // WIDE,)),
             dma((frames // ROWS,)), dma((frames // ROWS,)),
-            dma((3,)),
+            dma((4,)),
             dma((3, n_mp)), dma((n_mp,)), dma((n_mp,)), dma((n_mp,)),
             pltpu.SemaphoreType.REGULAR,
         ],
         compiler_params=pltpu.CompilerParams(
-            collective_id=0, has_side_effects=True, vmem_limit_bytes=48 * 2**20
+            collective_id=0, has_side_effects=True, vmem_limit_bytes=60 * 2**20
         ),
     )(frames_in, weight, conv_kernels[0], valid_length, out_cotangent)
     if not relay:

time: 153 us -> 144 us (0.941)
  Pallas kernels: 145 us -> 139 us
  local copies, waits for them, and re-layouts: 6.07 us -> 3.97 us
    pallas_call x1, Pallas kernels: 145 us -> 139 us  [on_device(): pl.pallas_call(functools.partial(cascade, relay), out_shape=(jax.ShapeDty...]
    unnamed x10 -> x4, local copies, waits for them, and re-layouts: 5.43 us -> 2.57 us
where the time goes in v2:
time: 144 us
  Pallas kernels  139 us (97%)
  local copies, waits for them, and re-layouts  3.97 us (3%)
    pallas_call x1, Pallas kernels, on_device(): pl.pallas_call(functools.partial(cascade, relay), out_shape=(jax.ShapeDty...  139 us

profile of v2, /device:TPU:0, one launch (start us, length us, event | category | flops | bytes accessed | tf_op | source)
XLA Modules:
  0.0 143.9 jit_solution(14397808880421815268)
XLA Ops:
  1.3 138.7 %shard_map.76 = (bf16[1,128,1536]{2,1,0:T(8,128)(2,1)}, bf16[1,128,1536]{2,1,0:T(8,128)(2,1)}, f32[1,31,192]{2,1,0:T(8,128)}) custom-call(bf16[128,1536]{1,0:T(8,128)(2,1)} %x_any.1, bf16[192,1536]{1,0:T(8,128)(2,1)} %bitcast.2, bf16[31,1536]{1,0:T(8,128)(2,1)} %bitcast.3, s32[1]{0:T(128)S(6)} %copy.11.vl_ref, bf16[128,1536]{1,0:T(8,128)(2,1)} %cot_any.1), custom_call_target="tpu_custom_call" | custom-call | tf_op jit(solution)/shard_map/pallas_call | solution.py:435
  140.0 1.4 copy.8
  141.4 0.0 copy-start
  141.4 1.8 %copy.12 = bf16[1,128,1536]{2,1,0:T(8,128)(2,1)} copy(bf16[1,128,1536]{2,1,0:T(8,128)(2,1)} %get-tuple-element.9) | data formatting | bytes 786432
  143.2 0.0 copy-done
  143.2 0.7 copy.13
Async XLA Ops:
  141.4 1.8 %copy-start = (bf16[1,128,1536]{2,1,0:T(8,128)(2,1)S(1)}, bf16[1,128,1536]{2,1,0:T(8,128)(2,1)}, u32[]{:S(2)}) copy-start(bf16[1,128,1536]{2,1,0:T(8,128)(2,1)} %get-tuple-element.10) | copy-start | bytes 1179652

commit v3 on v2

--- a/solution.py
+++ b/solution.py
@@ -22,7 +22,7 @@
     out_whole, gin_whole, kg_out,
     cur, up, norm, inv, pm, pg, act, slope, gs, w_ref, k_bf, k_ref, kg_ref, kg_land,
     halo_send, halo_recv, in_send, in_recv, up_send, up_recv,
-    local_sem, w_send, w_recv, kg_send, kg_recv, turn_sem,
+    local_sem, w_send, w_recv, end_send, end_recv, kg_send, kg_recv, turn_sem,
 ):
     out_ref, gin_ref = out_whole.at[0], gin_whole.at[0]
     frames, width = x_any.shape
@@ -64,13 +64,24 @@
     row, column = lax.div(mp, 2), lax.rem(mp, 2)
     n_row = n_mp // 2
 
-    def block_copy(block, way):
-        rows = pl.ds(pl.multiple_of(block * own, own), own)
+    half = own // 2
+
+    def block_copy(block, way, count=own):
+        rows = pl.ds(pl.multiple_of(block * own, own), count)
         target = (mp + 2, mp - 2, mp + 1 - 2 * column)[way]
         return pltpu.make_async_remote_copy(
             src_ref=w_ref.at[rows], dst_ref=w_ref.at[rows],
             send_sem=w_send.at[way, block], recv_sem=w_recv.at[block],
             device_id={"mp": target}, device_id_type=MESH,
+        )
+
+    def end_copy(way):
+        block = (0 if way == 0 else n_mp - 2) + 1 - column
+        rows = pl.ds(pl.multiple_of(block * own + half, half), half)
+        return pltpu.make_async_remote_copy(
+            src_ref=w_ref.at[rows], dst_ref=w_ref.at[rows],
+            send_sem=end_send.at[way], recv_sem=end_recv.at[way],
+            device_id={"mp": mp + 2 if way == 0 else mp - 2}, device_id_type=MESH,
         )
 
     def each_block(distance, act_on, arrive):
@@ -85,35 +96,61 @@
         def _():
             arrive(low)
             pl.when(row < n_row - 1)(lambda: act_on(low, 0))
-            act_on(low, 2)
+            pl.when(row == distance)(lambda: act_on(low, 2, half))
+            pl.when(row > distance)(lambda: act_on(low, 2))
 
         @pl.when(row + distance < n_row)
         def _():
             arrive(high)
             pl.when(row > 0)(lambda: act_on(high, 1))
-            act_on(high, 2)
+            pl.when(row + distance == n_row - 1)(lambda: act_on(high, 2, half))
+            pl.when(row + distance < n_row - 1)(lambda: act_on(high, 2))
 
     def pass_on(distance):
         each_block(
             distance,
-            lambda block, way: block_copy(block, way).start(),
+            lambda *what: block_copy(*what).start(),
             lambda block: block_copy(block, 0).wait_recv(),
         )
+        if distance == 1:
+            for way, end in ((0, 0), (1, n_row - 1)):
+
+                @pl.when(row == end)
+                def _():
+                    block_copy(2 * end + 1 - column, 2).wait_recv()
+                    end_copy(way).start()
 
     def passed():
         for distance in range(n_row):
             each_block(
                 distance,
-                lambda block, way: block_copy(block, way).wait_send(),
+                lambda *what: block_copy(*what).wait_send(),
                 lambda block: None,
             )
+        pl.when(row < n_row - 1)(lambda: end_copy(0).wait_send())
+        pl.when(row > 0)(lambda: end_copy(1).wait_send())
 
     def gather_rest(first):
         if relay:
             for distance in range(first, n_row):
                 pass_on(distance)
+
+            @pl.when(row > 0)
+            def _():
+                end_copy(0).wait_recv()
+                pl.when(row < n_row - 1)(lambda: end_copy(0).start())
+
+            @pl.when(row < n_row - 1)
+            def _():
+                end_copy(1).wait_recv()
+                pl.when(row > 0)(lambda: end_copy(1).start())
+
             for index in range(n_row):
-                block_copy(index * 2 + 1 - column, 2).wait_recv()
+                block = index * 2 + 1 - column
+                if index in (0, n_row - 1):
+                    pl.when(row != index)(lambda: block_copy(block, 2, half).wait_recv())
+                else:
+                    block_copy(block, 2).wait_recv()
 
     def kg_copy(target, sender):
         start = 384 * lax.div(target, 2) + 128 * lax.rem(target, 2)
@@ -460,7 +497,7 @@
             dma((width // WIDE,)), dma((width // WIDE,)),
             dma((frames // ROWS,)), dma((frames // ROWS,)),
             dma((4,)),
-            dma((3, n_mp)), dma((n_mp,)), dma((n_mp,)), dma((n_mp,)),
+            dma((3, n_mp)), dma((n_mp,)), dma((2,)), dma((2,)), dma((n_mp,)), dma((n_mp,)),
             pltpu.SemaphoreType.REGULAR,
         ],
         compiler_params=pltpu.CompilerParams(

time: 144 us -> 139 us (0.965)
  Pallas kernels: 139 us -> 133 us
    pallas_call x1, Pallas kernels: 139 us -> 133 us  [on_device(): pl.pallas_call(functools.partial(cascade, relay), out_shape=(jax.ShapeDty...]
where the time goes in v3:
time: 139 us; the launch traced here: 138 us
  Pallas kernels  133 us (96%)
  local copies, waits for them, and re-layouts  3.97 us (3%)
    pallas_call x1, Pallas kernels, on_device(): pl.pallas_call(functools.partial(cascade, relay), out_shape=(jax.ShapeDty...  133 us

profile of v3, /device:TPU:0, one launch (start us, length us, event | category | flops | bytes accessed | tf_op | source)
XLA Modules:
  0.0 138.4 jit_solution(12879974025409607932)
XLA Ops:
  1.3 133.1 %shard_map.76 = (bf16[1,128,1536]{2,1,0:T(8,128)(2,1)}, bf16[1,128,1536]{2,1,0:T(8,128)(2,1)}, f32[1,31,192]{2,1,0:T(8,128)}) custom-call(bf16[128,1536]{1,0:T(8,128)(2,1)} %x_any.1, bf16[192,1536]{1,0:T(8,128)(2,1)} %bitcast.2, bf16[31,1536]{1,0:T(8,128)(2,1)} %bitcast.3, s32[1]{0:T(128)S(6)} %copy.11.vl_ref, bf16[128,1536]{1,0:T(8,128)(2,1)} %cot_any.1), custom_call_target="tpu_custom_call" | custom-call | tf_op jit(solution)/shard_map/pallas_call | solution.py:472
  134.4 1.4 %copy.8 = f32[1,31,192]{2,0,1:T(1,128)} copy(f32[1,31,192]{2,1,0:T(8,128)} %get-tuple-element.5) | data formatting | bytes 47616 | tf_op jit(solution)/shard_map/pallas_call | solution.py:472
  135.8 0.0 copy-start
  135.8 1.8 %copy.12 = bf16[1,128,1536]{2,1,0:T(8,128)(2,1)} copy(bf16[1,128,1536]{2,1,0:T(8,128)(2,1)} %get-tuple-element.9) | data formatting | bytes 786432
  137.6 0.0 copy-done
  137.6 0.7 copy.13
Async XLA Ops:
  135.8 1.8 %copy-start = (bf16[1,128,1536]{2,1,0:T(8,128)(2,1)S(1)}, bf16[1,128,1536]{2,1,0:T(8,128)(2,1)}, u32[]{:S(2)}) copy-start(bf16[1,128,1536]{2,1,0:T(8,128)(2,1)} %get-tuple-element.10) | copy-start | bytes 1179652

commit v4 on v3

--- a/solution.py
+++ b/solution.py
@@ -20,11 +20,10 @@
 def cascade(
     relay, x_any, w_any, k_any, vl_ref, cot_any,
     out_whole, gin_whole, kg_out,
-    cur, up, norm, inv, pm, pg, act, slope, gs, w_ref, k_bf, k_ref, kg_ref, kg_land,
+    cur, up, norm, inv, pm, pg, act, slope, gs, out_ref, gin_ref, w_ref, k_bf, k_ref, kg_ref, kg_land,
     halo_send, halo_recv, in_send, in_recv, up_send, up_recv,
     local_sem, w_send, w_recv, end_send, end_recv, kg_send, kg_recv, turn_sem,
 ):
-    out_ref, gin_ref = out_whole.at[0], gin_whole.at[0]
     frames, width = x_any.shape
     taps = k_ref.shape[0]
     seg, mp = lax.axis_index("segment"), lax.axis_index("mp")
@@ -48,6 +47,8 @@
     x_copy = pltpu.make_async_copy(x_any, cur, local_sem.at[1])
     cot_copy = pltpu.make_async_copy(cot_any, up, local_sem.at[2])
     k_copy = pltpu.make_async_copy(k_any, k_bf, local_sem.at[3])
+    out_copy = pltpu.make_async_copy(out_ref, out_whole.at[0], local_sem.at[4])
+    gin_copy = pltpu.make_async_copy(gin_ref, gin_whole.at[0], local_sem.at[5])
     w_copy.start()
     k_copy.start()
 
@@ -351,6 +352,8 @@
         @pl.when(seg < n_seg - 1)
         def _():
             in_copy(tile).start()
+
+    out_copy.start()
 
     @pl.when(seg < n_seg - 1)
     def _():
@@ -421,6 +424,8 @@
         def _():
             up_copy(block).start()
 
+    gin_copy.start()
+
     @pl.when(seg > 0)
     def _():
         tap_grads()
@@ -440,6 +445,8 @@
     else:
         kg_out[0] = kg_ref[:taps, :]
 
+    out_copy.wait()
+    gin_copy.wait()
     halo_sent(pm, 0)
     halo_sent(pg, 2)
 
@@ -477,7 +484,7 @@
             jax.ShapeDtypeStruct((1, taps, own if relay else width), F32),
         ),
         in_specs=[whole, whole, whole, smem, whole],
-        out_specs=(vmem, vmem, vmem),
+        out_specs=(whole, whole, vmem),
         scratch_shapes=[
             pltpu.VMEM((frames, width), BF),
             pltpu.VMEM((frames, width), BF),
@@ -488,6 +495,8 @@
             pltpu.VMEM((frames, width), BF),
             pltpu.VMEM((frames, width), F32),
             pltpu.VMEM((frames, width), F32),
+            pltpu.VMEM((frames, width), BF),
+            pltpu.VMEM((frames, width), BF),
             pltpu.VMEM((width, width), BF),
             pltpu.VMEM((taps, width), BF),
             pltpu.VMEM((taps, width), F32),
@@ -496,7 +505,7 @@
             dma((4,)), dma((4,)),
             dma((width // WIDE,)), dma((width // WIDE,)),
             dma((frames // ROWS,)), dma((frames // ROWS,)),
-            dma((4,)),
+            dma((6,)),
             dma((3, n_mp)), dma((n_mp,)), dma((2,)), dma((2,)), dma((n_mp,)), dma((n_mp,)),
             pltpu.SemaphoreType.REGULAR,
         ],

time: 139 us -> 138 us (level)
  no operation moved by 1% of the time
where the time goes in v4:
time: 138 us
  Pallas kernels  133 us (96%)
  local copies, waits for them, and re-layouts  3.97 us (3%)
    pallas_call x1, Pallas kernels, on_device(): pl.pallas_call(functools.partial(cascade, relay), out_shape=(jax.ShapeDty...  133 us

profile of v4, /device:TPU:0, one launch (start us, length us, event | category | flops | bytes accessed | tf_op | source)
XLA Modules:
  0.0 138.2 jit_solution(6818531416846659945)
XLA Ops:
  1.3 133.0 %shard_map.76 = (bf16[1,128,1536]{2,1,0:T(8,128)(2,1)}, bf16[1,128,1536]{2,1,0:T(8,128)(2,1)}, f32[1,31,192]{2,1,0:T(8,128)}) custom-call(bf16[128,1536]{1,0:T(8,128)(2,1)} %x_any.1, bf16[192,1536]{1,0:T(8,128)(2,1)} %bitcast.2, bf16[31,1536]{1,0:T(8,128)(2,1)} %bitcast.3, s32[1]{0:T(128)S(6)} %copy.11.vl_ref, bf16[128,1536]{1,0:T(8,128)(2,1)} %cot_any.1), custom_call_target="tpu_custom_call" | custom-call | tf_op jit(solution)/shard_map/pallas_call | solution.py:479
  134.3 1.4 %copy.8 = f32[1,31,192]{2,0,1:T(1,128)} copy(f32[1,31,192]{2,1,0:T(8,128)} %get-tuple-element.5) | data formatting | bytes 47616 | tf_op jit(solution)/shard_map/pallas_call | solution.py:479
  135.7 0.0 copy-start
  135.7 1.8 %copy.12 = bf16[1,128,1536]{2,1,0:T(8,128)(2,1)} copy(bf16[1,128,1536]{2,1,0:T(8,128)(2,1)} %get-tuple-element.9) | data formatting | bytes 786432
  137.5 0.0 copy-done
  137.5 0.7 copy.13
Async XLA Ops:
  135.7 1.8 %copy-start = (bf16[1,128,1536]{2,1,0:T(8,128)(2,1)S(1)}, bf16[1,128,1536]{2,1,0:T(8,128)(2,1)}, u32[]{:S(2)}) copy-start(bf16[1,128,1536]{2,1,0:T(8,128)(2,1)} %get-tuple-element.10) | copy-start | bytes 1179652

commit v5 on v3

--- a/solution.py
+++ b/solution.py
@@ -301,6 +301,12 @@
         def _():
             pass_on(1)
 
+        @pl.when(seg == 0)
+        def _():
+            pl.semaphore_signal(
+                turn_sem, inc=1, device_id={"segment": seg + 1}, device_id_type=MESH
+            )
+
     halo_wait(pm, 0)
 
     def shifted(padded):
@@ -332,12 +338,6 @@
         @pl.when(seg < 2)
         def _():
             pass_on(2)
-
-        @pl.when(seg == 0)
-        def _():
-            pl.semaphore_signal(
-                turn_sem, inc=1, device_id={"segment": seg + 1}, device_id_type=MESH
-            )
 
         @pl.when(seg < 2)
         def _():

time: 139 us -> 141 us (1.014)
  Pallas kernels: 133 us -> 136 us
    pallas_call x1, Pallas kernels: 133 us -> 136 us  [on_device(): pl.pallas_call(functools.partial(cascade, relay), out_shape=(jax.ShapeDty...]
where the time goes in v5:
time: 141 us
  Pallas kernels  136 us (96%)
  local copies, waits for them, and re-layouts  3.97 us (3%)
    pallas_call x1, Pallas kernels, on_device(): pl.pallas_call(functools.partial(cascade, relay), out_shape=(jax.ShapeDty...  136 us

profile of v5, /device:TPU:0, one launch (start us, length us, event | category | flops | bytes accessed | tf_op | source)
XLA Modules:
  0.0 140.9 jit_solution(9842864801445226221)
XLA Ops:
  1.3 135.7 %shard_map.76 = (bf16[1,128,1536]{2,1,0:T(8,128)(2,1)}, bf16[1,128,1536]{2,1,0:T(8,128)(2,1)}, f32[1,31,192]{2,1,0:T(8,128)}) custom-call(bf16[128,1536]{1,0:T(8,128)(2,1)} %x_any.1, bf16[192,1536]{1,0:T(8,128)(2,1)} %bitcast.2, bf16[31,1536]{1,0:T(8,128)(2,1)} %bitcast.3, s32[1]{0:T(128)S(6)} %copy.11.vl_ref, bf16[128,1536]{1,0:T(8,128)(2,1)} %cot_any.1), custom_call_target="tpu_custom_call" | custom-call | tf_op jit(solution)/shard_map/pallas_call | solution.py:472
  137.0 1.4 copy.8
  138.4 0.0 copy-start
  138.4 1.8 %copy.12 = bf16[1,128,1536]{2,1,0:T(8,128)(2,1)} copy(bf16[1,128,1536]{2,1,0:T(8,128)(2,1)} %get-tuple-element.9) | data formatting | bytes 786432
  140.2 0.0 copy-done
  140.2 0.7 copy.13
Async XLA Ops:
  138.4 1.8 %copy-start = (bf16[1,128,1536]{2,1,0:T(8,128)(2,1)S(1)}, bf16[1,128,1536]{2,1,0:T(8,128)(2,1)}, u32[]{:S(2)}) copy-start(bf16[1,128,1536]{2,1,0:T(8,128)(2,1)} %get-tuple-element.10) | copy-start | bytes 1179652
